TPU v7x, 256 devices: a whole 4x4x8 slice. The times are simulated.
256 devices in a mesh: row: 16 (over y, x), col: 16 (over z, core).
Axes of the slice: x: 4, y: 4, z: 8, core: 2. Of those that a mesh axis runs over, the one named last changes fastest.
Arguments:
- source: float32 [2048, 64, 128], P(('row', 'col')), may hold values from -6 to 6
- blocks: float32 [65536, 64, 64], P(('row', 'col')), may hold values from -0.15625 to 0.15625
- row_index: int32 [65536], P(('row', 'col')), may hold values from 0 to 127
- col_index: int32 [65536], P(('row', 'col')), may hold values from 0 to 127
- live_count: int32 [256], P(('row', 'col')), may hold values from 64 to 256, as said below
Outputs:
- irradiance: float32 [2048, 64, 128], P(('row', 'col'))
Inputs may be any that keep to these rules, and one draw needn't show every extreme that they name: `live_count`: slots of a device beyond its live count are padding; some device has all 256 slots live.
All inputs are finite; a program needn't handle non-finite values.
Results may differ from a plain program's by a relative error of at most 0.0003.
Values sent between devices are 32-bit elements; how exact they have to be, the bound alone decides.
A program may use at most 128 MiB of HBM per device.

v0:
```python
import jax
import jax.numpy as jnp
from jax import lax
from jax.sharding import PartitionSpec as P

ITERS = 2


def local_transfer(blocks, gathered, row_ids, col_index, group_rows):
    picked = jnp.take(gathered, col_index, axis=0)
    products = jnp.einsum("nij,njl->nil", blocks, picked, precision=lax.Precision.HIGHEST)
    summed = jax.ops.segment_sum(products, row_ids, num_segments=group_rows + 1)
    return summed[:group_rows]


def body(source, blocks, row_index, col_index, live_count):
    bricks_here = source.shape[0]
    group_rows = bricks_here * lax.axis_size("col")
    live_total = live_count[0]
    slot_ids = jnp.arange(blocks.shape[0], dtype=jnp.int32)
    row_ids = jnp.where(slot_ids < live_total, row_index, group_rows)
    field = source
    for bounce in range(ITERS):
        gathered = lax.all_gather(field, "row", axis=0, tiled=True)
        partial_value = local_transfer(blocks, gathered, row_ids, col_index, group_rows)
        whole = lax.psum(partial_value, "col")
        owned = lax.dynamic_slice_in_dim(whole, lax.axis_index("col") * bricks_here, bricks_here, 0)
        field = source + owned
    return field


def solution(mesh):
    in_specs = (
        P(("row", "col"), None, None),
        P(("row", "col"), None, None),
        P(("row", "col")),
        P(("row", "col")),
        P(("row", "col")),
    )
    out_specs = P(("row", "col"), None, None)
    return jax.shard_map(body, mesh=mesh, in_specs=in_specs, out_specs=out_specs, check_vma=False)
```

profile of v0, /device:TPU:1, one launch (start us, length us, event | category | flops | bytes accessed | tf_op | source)
XLA Modules:
  0.0 516.3 jit_solution(3725218833665404875)
XLA Ops:
  6.5 0.0 copy-start.1
  6.5 0.0 copy-start.2
  6.5 0.0 all-gather.3.cloned.1.call-start
  6.5 0.7 all-gather.3.cloned.1.call-update
  7.3 0.0 all-reduce.3.cloned.1.call-start
  7.3 9.2 %copy.7 = f32[256,64,64]{2,1,0:T(8,128)} copy(f32[256,64,64]{0,2,1:T(8,128)} %param.8) | data formatting | bytes 8388608 | tf_op args[1]
  17.1 0.0 copy-done.1
  17.2 0.0 copy-done.2
  17.2 52.7 %all-gather.3.cloned.1.call-done = f32[128,64,128]{2,1,0:T(8,128)} async-done(((f32[8,64,128]{2,1,0:T(8,128)}), f32[128,64,128]{2,1,0:T(8,128)}) %all-gather.3.cloned.1.call-update) | async-done | bytes 4194320 | tf_op jit(solution)/shard_map/all_gather | solution.py:24
  69.8 6.5 %gather_fusion = f32[256,64,128]{2,1,0:T(8,128)} fusion(f32[128,64,128]{2,1,0:T(8,128)} %all-gather.3.cloned.1.call-done, s32[1024]{0:T(1024)S(1)} %pad_clamp_fusion), kind=kCustom, calls=%fused_computation.clone | custom fusion | bytes 16778240 | tf_op jit(solution)/shard_map/jit(_take)/gather | solution.py:10
  76.3 14.7 %fusion.8 = f32[256,64,128]{2,1,0:T(8,128)} fusion(f32[256,64,64]{2,1,0:T(8,128)} %copy.7, f32[256,64,128]{2,1,0:T(8,128)} %gather_fusion, pred[256]{0:T(512)(128)(4,1)S(1)} %compare_and_fusion), kind=kOutput, calls=%fused_computation.12 | convolution fusion | flops 1612709888 | bytes 20971776 | tf_op jit(solution)/shard_map/nij,njl->nil/dot_general | solution.py:11
  91.0 2.5 broadcast.6.clone
  93.5 39.8 %scatter_fusion = f32[129,64,128]{2,1,0:T(8,128)} fusion(f32[129,64,128]{2,1,0:T(8,128)} %broadcast.6.clone, s32[256]{0:T(256)S(1)} %compare_select_fusion.1, f32[256,64,128]{2,1,0:T(8,128)} %fusion.8), kind=kCustom, calls=%fused_computation.2 | custom fusion | flops 2097152 | bytes 25166848 | tf_op jit(solution)/shard_map/scatter-add | solution.py:12
  133.3 0.0 copy-start
  133.3 4.8 slice.12
  138.1 0.0 all-reduce.3.cloned.1.call-update
  138.1 0.0 all-gather.5.cloned.1.call-start
  138.1 121.1 %all-reduce.3.cloned.1.call-done = f32[128,64,128]{2,1,0:T(8,128)} async-done(((f32[128,64,128]{2,1,0:T(8,128)}), f32[128,64,128]{2,1,0:T(8,128)}) %all-reduce.3.cloned.1.call-update) | async-done | bytes 4194320 | tf_op jit(solution)/shard_map/psum | solution.py:26
  259.3 0.0 copy-done
  259.3 1.7 dynamic-slice_add_fusion.1
  261.0 0.0 all-gather.5.cloned.1.call-update
  261.0 0.2 all-reduce.5.cloned.1.call-start
  261.2 57.4 %all-gather.5.cloned.1.call-done = f32[128,64,128]{2,1,0:T(8,128)} async-done(((f32[8,64,128]{2,1,0:T(8,128)}), f32[128,64,128]{2,1,0:T(8,128)}) %all-gather.5.cloned.1.call-update) | async-done | bytes 4194320 | tf_op jit(solution)/shard_map/all_gather | solution.py:24
  318.6 6.5 %gather_fusion.1 = f32[256,64,128]{2,1,0:T(8,128)} fusion(f32[128,64,128]{2,1,0:T(8,128)} %all-gather.5.cloned.1.call-done, s32[1024]{0:T(1024)S(1)} %pad_clamp_fusion), kind=kCustom, calls=%fused_computation.1.clone | custom fusion | bytes 16778240 | tf_op jit(solution)/shard_map/jit(_take)/gather | solution.py:10
  325.1 14.7 %fusion.11 = f32[256,64,128]{2,1,0:T(8,128)} fusion(f32[256,64,64]{2,1,0:T(8,128)} %copy.7, f32[256,64,128]{2,1,0:T(8,128)} %gather_fusion.1, pred[256]{0:T(512)(128)(4,1)S(1)} %compare_and_fusion), kind=kOutput, calls=%fused_computation.13 | convolution fusion | flops 1612709888 | bytes 20971776 | tf_op jit(solution)/shard_map/nij,njl->nil/dot_general | solution.py:11
  339.8 2.5 broadcast.6
  342.3 39.8 %scatter_fusion.1 = f32[129,64,128]{2,1,0:T(8,128)} fusion(f32[129,64,128]{2,1,0:T(8,128)} %broadcast.6, s32[256]{0:T(256)S(1)} %compare_select_fusion.1, f32[256,64,128]{2,1,0:T(8,128)} %fusion.11), kind=kCustom, calls=%fused_computation.3 | custom fusion | flops 2097152 | bytes 25166848 | tf_op jit(solution)/shard_map/scatter-add | solution.py:12
  382.1 4.8 slice.13
  386.8 0.0 all-reduce.5.cloned.1.call-update
  386.9 121.2 %all-reduce.5.cloned.1.call-done = f32[128,64,128]{2,1,0:T(8,128)} async-done(((f32[128,64,128]{2,1,0:T(8,128)}), f32[128,64,128]{2,1,0:T(8,128)}) %all-reduce.5.cloned.1.call-update) | async-done | bytes 4194320 | tf_op jit(solution)/shard_map/psum | solution.py:26
  508.1 1.7 dynamic-slice_add_fusion
  (4 shorter events, 0.0 us)
Async XLA Ops:
  6.5 10.6 %copy-start.1 = (s32[256]{0:T(256)S(1)}, s32[256]{0:T(256)}, u32[]{:S(2)}) copy-start(s32[256]{0:T(256)} %param.10) | copy-start | bytes 3076
  6.5 10.6 %copy-start.2 = (s32[256]{0:T(256)S(1)}, s32[256]{0:T(256)}, u32[]{:S(2)}) copy-start(s32[256]{0:T(256)} %param.9) | copy-start | bytes 3076
  6.5 63.3 %all-gather.3.cloned.1.call-start = ((), (), s32[]{:S(2)}) async-start(), calls=%async_computation | async-start | bytes 4456448 | tf_op jit(solution)/shard_map/all_gather | solution.py:24
  7.3 252.0 %all-reduce.3.cloned.1.call-start = ((), (), s32[]{:S(2)}) async-start(), calls=%async_computation.1 | async-start | bytes 8388608 | tf_op jit(solution)/shard_map/psum | solution.py:26
  133.3 126.0 %copy-start = (f32[8,64,128]{2,1,0:T(8,128)S(1)}, f32[8,64,128]{2,1,0:T(8,128)}, u32[]{:S(2)}) copy-start(f32[8,64,128]{2,1,0:T(8,128)} %param.7) | copy-start | bytes 786436
  138.1 180.5 %all-gather.5.cloned.1.call-start = ((), (), s32[]{:S(2)}) async-start(), calls=%async_computation.2 | async-start | bytes 4456448 | tf_op jit(solution)/shard_map/all_gather | solution.py:24
  261.0 247.1 %all-reduce.5.cloned.1.call-start = ((), (), s32[]{:S(2)}) async-start(), calls=%async_computation.3 | async-start | bytes 8388608 | tf_op jit(solution)/shard_map/psum | solution.py:26
Sparse Core Ops, SparseCore 0:
  9.8 60.0 all-gather.2
  138.2 121.0 all-reduce.2
  261.7 56.8 all-gather.4
  387.0 121.0 all-reduce.4
where the time goes:
time: 518 us; the launch traced here: 516 us
  waiting for transfers between devices  353 us (68%)
  other arithmetic  83 us (16%)
  local copies, waits for them, and re-layouts  36.6 us (7%)
  matrix products  29.3 us (6%)
  between operations  13.8 us (3%)
    psum x2, waiting for transfers between devices, body(): whole = lax.psum(partial_value, 'col')  242 us
    all_gather x2, waiting for transfers between devices, body(): gathered = lax.all_gather(field, 'row', axis=0, tiled=True)  110 us
    scatter-add x2, other arithmetic, local_transfer(): summed = jax.ops.segment_sum(products, row_ids, num_segments=group_rows + 1)  79.7 us
    dot_general x2, matrix products, local_transfer(): jnp.einsum('nij,njl->nil', blocks, picked, precision=lax.Precision.HIGHEST)  29.3 us
    gather x2, local copies, waits for them, and re-layouts, local_transfer(): picked = jnp.take(gathered, col_index, axis=0)  13 us
  transfers between devices with their start and end apart: 4, of which 4 were waited for; matrix products, arithmetic and copies ran while one was open for 2% of the time, Pallas kernels for 0%

commit v1 on v0

--- a/solution.py
+++ b/solution.py
@@ -4,6 +4,15 @@
 from jax.sharding import PartitionSpec as P
 
 ITERS = 2
+
+
+def added_up(block, axis):
+    devices = lax.axis_size(axis)
+    total, reach = (block, 1)
+    while reach < devices:
+        total = total + lax.ppermute(total, axis, [(i, i ^ reach) for i in range(devices)])
+        reach = 2 * reach
+    return total
 
 
 def local_transfer(blocks, gathered, row_ids, col_index, group_rows):
@@ -23,7 +32,7 @@
     for bounce in range(ITERS):
         gathered = lax.all_gather(field, "row", axis=0, tiled=True)
         partial_value = local_transfer(blocks, gathered, row_ids, col_index, group_rows)
-        whole = lax.psum(partial_value, "col")
+        whole = added_up(partial_value, "col")
         owned = lax.dynamic_slice_in_dim(whole, lax.axis_index("col") * bricks_here, bricks_here, 0)
         field = source + owned
     return field

time: 518 us -> 1220 us (2.36)
  waiting for transfers between devices: 353 us -> 1020 us
  starting transfers between devices: 0.31 us -> 21.9 us
    ppermute x0 -> x8, waiting for transfers between devices: none -> 916 us  [added_up(): lax.ppermute(total, axis, [(i, i ^ reach) for i in range(devices)])]
    psum x2 -> x0, waiting for transfers between devices: 242 us -> none  [body(): whole = lax.psum(partial_value, 'col')]
    ppermute x0 -> x8, starting transfers between devices: none -> 21.8 us  [added_up(): lax.ppermute(total, axis, [(i, i ^ reach) for i in range(devices)])]
  transfers between devices with their start and end apart: 4 -> 10, of which waited for: 4 -> 10; matrix products, arithmetic and copies ran while one was open for 2% -> 1% of each run, Pallas kernels for 0% -> 0%
where the time goes in v1:
time: 1220 us; the launch traced here: 1210 us
  waiting for transfers between devices  1020 us (84%)
  other arithmetic  91.7 us (8%)
  local copies, waits for them, and re-layouts  32.5 us (3%)
  matrix products  29.3 us (2%)
  starting transfers between devices  21.9 us (2%)
  between operations  14.2 us (1%)
    ppermute x8, waiting for transfers between devices, added_up(): lax.ppermute(total, axis, [(i, i ^ reach) for i in range(devices)])  916 us
    all_gather x2, waiting for transfers between devices, body(): gathered = lax.all_gather(field, 'row', axis=0, tiled=True)  108 us
    scatter-add x2, other arithmetic, local_transfer(): summed = jax.ops.segment_sum(products, row_ids, num_segments=group_rows + 1)  79.5 us
    dot_general x2, matrix products, local_transfer(): jnp.einsum('nij,njl->nil', blocks, picked, precision=lax.Precision.HIGHEST)  29.3 us
  transfers between devices with their start and end apart: 10, of which 10 were waited for; matrix products, arithmetic and copies ran while one was open for 1% of the time, Pallas kernels for 0%

profile of v1, /device:TPU:1, one launch (start us, length us, event | category | flops | bytes accessed | tf_op | source)
XLA Modules:
  0.0 1213.7 jit_solution(4371542085471074887)
XLA Ops:
  7.3 9.2 copy.8
  17.2 52.6 %all-gather.3.cloned.1.call-done = f32[128,64,128]{2,1,0:T(8,128)} async-done(((f32[8,64,128]{2,1,0:T(8,128)}), f32[128,64,128]{2,1,0:T(8,128)}) %all-gather.3.cloned.1.call-update) | async-done | bytes 4194320 | tf_op jit(solution)/shard_map/all_gather | solution.py:33
  69.8 6.5 gather_fusion
  76.3 14.6 %fusion.8 = f32[256,64,128]{2,1,0:T(8,128)} fusion(f32[256,64,64]{2,1,0:T(8,128)} %copy.8, f32[256,64,128]{2,1,0:T(8,128)} %gather_fusion, pred[256]{0:T(512)(128)(4,1)S(1)} %compare_and_fusion), kind=kOutput, calls=%fused_computation.12 | convolution fusion | flops 1612709888 | bytes 20971776 | tf_op jit(solution)/shard_map/nij,njl->nil/dot_general | solution.py:20
  91.0 2.5 broadcast.6.clone
  93.5 39.7 %scatter_fusion = f32[129,64,128]{2,1,0:T(8,128)} fusion(f32[129,64,128]{2,1,0:T(8,128)} %broadcast.6.clone, s32[256]{0:T(256)S(1)} %compare_select_fusion.1, f32[256,64,128]{2,1,0:T(8,128)} %fusion.8), kind=kCustom, calls=%fused_computation.2 | custom fusion | flops 2097152 | bytes 25166848 | tf_op jit(solution)/shard_map/scatter-add | solution.py:21
  133.2 2.7 slice.12
  136.4 6.8 collective-permute-done
  143.2 1.4 slice_add_fusion.1
  144.6 1.4 collective-permute-start.1
  146.0 90.4 %collective-permute-done.1 = f32[128,64,128]{2,1,0:T(8,128)S(1)} collective-permute-done((f32[128,64,128]{2,1,0:T(8,128)S(1)}, f32[128,64,128]{2,1,0:T(8,128)S(1)}, u32[]{:S(2)}, u32[]{:S(2)}) %collective-permute-start.1) | collective-permute-done | bytes 4194336 | tf_op jit(solution)/shard_map/ppermute | solution.py:13
  236.4 1.4 add.45
  237.8 3.1 collective-permute-start.2
  240.9 180.0 %collective-permute-done.2 = f32[128,64,128]{2,1,0:T(8,128)S(1)} collective-permute-done((f32[128,64,128]{2,1,0:T(8,128)S(1)}, f32[128,64,128]{2,1,0:T(8,128)S(1)}, u32[]{:S(2)}, u32[]{:S(2)}) %collective-permute-start.2) | collective-permute-done | bytes 4194336 | tf_op jit(solution)/shard_map/ppermute | solution.py:13
  420.9 2.9 add.46
  423.8 5.9 collective-permute-start.3
  429.7 180.9 %collective-permute-done.3 = f32[128,64,128]{2,1,0:T(8,128)} collective-permute-done((f32[128,64,128]{2,1,0:T(8,128)}, f32[128,64,128]{2,1,0:T(8,128)}, u32[]{:S(2)}, u32[]{:S(2)}) %collective-permute-start.3) | collective-permute-done | bytes 4194336 | tf_op jit(solution)/shard_map/ppermute | solution.py:13
  610.6 1.8 fusion.15
  612.4 55.2 %all-gather.5.cloned.1.call-done = f32[128,64,128]{2,1,0:T(8,128)} async-done(((f32[8,64,128]{2,1,0:T(8,128)}), f32[128,64,128]{2,1,0:T(8,128)}) %all-gather.5.cloned.1.call-update) | async-done | bytes 4194320 | tf_op jit(solution)/shard_map/all_gather | solution.py:33
  667.6 6.5 gather_fusion.1
  674.1 14.6 %fusion.11 = f32[256,64,128]{2,1,0:T(8,128)} fusion(f32[256,64,64]{2,1,0:T(8,128)} %copy.8, f32[256,64,128]{2,1,0:T(8,128)} %gather_fusion.1, pred[256]{0:T(512)(128)(4,1)S(1)} %compare_and_fusion), kind=kOutput, calls=%fused_computation.13 | convolution fusion | flops 1612709888 | bytes 20971776 | tf_op jit(solution)/shard_map/nij,njl->nil/dot_general | solution.py:20
  688.8 2.5 broadcast.6
  691.3 39.7 %scatter_fusion.1 = f32[129,64,128]{2,1,0:T(8,128)} fusion(f32[129,64,128]{2,1,0:T(8,128)} %broadcast.6, s32[256]{0:T(256)S(1)} %compare_select_fusion.1, f32[256,64,128]{2,1,0:T(8,128)} %fusion.11), kind=kCustom, calls=%fused_computation.3 | custom fusion | flops 2097152 | bytes 25166848 | tf_op jit(solution)/shard_map/scatter-add | solution.py:21
  731.0 2.7 slice.13
  734.2 6.8 collective-permute-done.4
  740.9 1.4 slice_add_fusion
  742.3 1.4 collective-permute-start.5
  743.7 90.4 %collective-permute-done.5 = f32[128,64,128]{2,1,0:T(8,128)S(1)} collective-permute-done((f32[128,64,128]{2,1,0:T(8,128)S(1)}, f32[128,64,128]{2,1,0:T(8,128)S(1)}, u32[]{:S(2)}, u32[]{:S(2)}) %collective-permute-start.5) | collective-permute-done | bytes 4194336 | tf_op jit(solution)/shard_map/ppermute | solution.py:13
  835.5 3.0 collective-permute-start.6
  838.6 180.0 %collective-permute-done.6 = f32[128,64,128]{2,1,0:T(8,128)S(1)} collective-permute-done((f32[128,64,128]{2,1,0:T(8,128)S(1)}, f32[128,64,128]{2,1,0:T(8,128)S(1)}, u32[]{:S(2)}, u32[]{:S(2)}) %collective-permute-start.6) | collective-permute-done | bytes 4194336 | tf_op jit(solution)/shard_map/ppermute | solution.py:13
  1019.9 5.8 collective-permute-start.7
  1025.8 180.4 %collective-permute-done.7 = f32[128,64,128]{2,1,0:T(8,128)S(1)} collective-permute-done((f32[128,64,128]{2,1,0:T(8,128)S(1)}, f32[128,64,128]{2,1,0:T(8,128)S(1)}, u32[]{:S(2)}, u32[]{:S(2)}) %collective-permute-start.7) | collective-permute-done | bytes 4194336 | tf_op jit(solution)/shard_map/ppermute | solution.py:13
  (23 shorter events, 5.3 us)
Async XLA Ops:
  6.5 63.3 %all-gather.3.cloned.1.call-start = ((), (), s32[]{:S(2)}) async-start(), calls=%async_computation | async-start | bytes 4456448 | tf_op jit(solution)/shard_map/all_gather | solution.py:33
  7.3 9.9 copy-start.3
  7.3 9.9 copy-start.4
  7.3 660.3 %all-gather.5.cloned.1.call-start = ((), (), s32[]{:S(2)}) async-start(), calls=%async_computation.1 | async-start | bytes 4456448 | tf_op jit(solution)/shard_map/all_gather | solution.py:33
  133.2 10.0 copy-start.1
  135.9 7.3 collective-permute-start
  144.6 91.8 %collective-permute-start.1 = (f32[128,64,128]{2,1,0:T(8,128)S(1)}, f32[128,64,128]{2,1,0:T(8,128)S(1)}, u32[]{:S(2)}, u32[]{:S(2)}) collective-permute-start(f32[128,64,128]{2,1,0:T(8,128)S(1)} %slice_add_fusion.1), channel_id=1, source_target_pairs={{0,2},{1,3},{2,0},{3,1},{4,6},{5,7},{6,4},{7,5},{8,10},{9,11},{10,... | collective-permute-start | bytes 12582920 | tf_op jit(solution)/shard_map/ppermute | solution.py:13
  237.8 372.9 %copy-start.2 = (f32[8,64,128]{2,1,0:T(8,128)S(1)}, f32[8,64,128]{2,1,0:T(8,128)}, u32[]{:S(2)}) copy-start(f32[8,64,128]{2,1,0:T(8,128)} %param.7) | copy-start | bytes 786436
  237.8 183.1 %collective-permute-start.2 = (f32[128,64,128]{2,1,0:T(8,128)S(1)}, f32[128,64,128]{2,1,0:T(8,128)S(1)}, u32[]{:S(2)}, u32[]{:S(2)}) collective-permute-start(f32[128,64,128]{2,1,0:T(8,128)S(1)} %add.45), channel_id=1, source_target_pairs={{0,4},{1,5},{2,6},{3,7},{4,0},{5,1},{6,2},{7,3},{8,12},{9,13},{10,... | collective-permute-start | bytes 12582920 | tf_op jit(solution)/shard_map/ppermute | solution.py:13
  423.8 186.8 %collective-permute-start.3 = (f32[128,64,128]{2,1,0:T(8,128)}, f32[128,64,128]{2,1,0:T(8,128)}, u32[]{:S(2)}, u32[]{:S(2)}) collective-permute-start(f32[128,64,128]{2,1,0:T(8,128)} %add.46), channel_id=1, source_target_pairs={{0,8},{1,9},{2,10},{3,11},{4,12},{5,13},{6,14},{7,15},{8,0},{9,1},... | collective-permute-start | bytes 12582920 | tf_op jit(solution)/shard_map/ppermute | solution.py:13
  731.0 9.9 copy-start
  733.7 7.3 collective-permute-start.4
  742.3 91.8 %collective-permute-start.5 = (f32[128,64,128]{2,1,0:T(8,128)S(1)}, f32[128,64,128]{2,1,0:T(8,128)S(1)}, u32[]{:S(2)}, u32[]{:S(2)}) collective-permute-start(f32[128,64,128]{2,1,0:T(8,128)S(1)} %slice_add_fusion), channel_id=1, source_target_pairs={{0,2},{1,3},{2,0},{3,1},{4,6},{5,7},{6,4},{7,5},{8,10},{9,11},{10,... | collective-permute-start | bytes 12582920 | tf_op jit(solution)/shard_map/ppermute | solution.py:13
  835.5 183.0 %collective-permute-start.6 = (f32[128,64,128]{2,1,0:T(8,128)S(1)}, f32[128,64,128]{2,1,0:T(8,128)S(1)}, u32[]{:S(2)}, u32[]{:S(2)}) collective-permute-start(f32[128,64,128]{2,1,0:T(8,128)S(1)} %add.51), channel_id=1, source_target_pairs={{0,4},{1,5},{2,6},{3,7},{4,0},{5,1},{6,2},{7,3},{8,12},{9,13},{10,... | collective-permute-start | bytes 12582920 | tf_op jit(solution)/shard_map/ppermute | solution.py:13
  1019.9 186.2 %collective-permute-start.7 = (f32[128,64,128]{2,1,0:T(8,128)S(1)}, f32[128,64,128]{2,1,0:T(8,128)S(1)}, u32[]{:S(2)}, u32[]{:S(2)}) collective-permute-start(f32[128,64,128]{2,1,0:T(8,128)S(1)} %add.52), channel_id=1, source_target_pairs={{0,8},{1,9},{2,10},{3,11},{4,12},{5,13},{6,14},{7,15},{8,0},{9,1},... | collective-permute-start | bytes 12582920 | tf_op jit(solution)/shard_map/ppermute | solution.py:13
Sparse Core Ops, SparseCore 0:
  9.8 60.0 all-gather.2
  612.5 55.0 all-gather.4
